TPU v7x, 32 devices: a whole 2x2x4 slice. The times are simulated.
32 devices in a mesh: rows: 8 (over y, x, core), cols: 4 (over z).
Axes of the slice: x: 2, y: 2, z: 4, core: 2. Of those that a mesh axis runs over, the one named last changes fastest.
Arguments:
- panel: float32 [2048, 256], P(('rows', 'cols')), may hold values from -1 to 1, as said below
- trailing: float32 [2048, 2048], P('rows', 'cols'), may hold values from -6 to 6
Outputs:
- r_factor: float32 [256, 256], replicated
- coefficients: float32 [256, 2048], P(None, 'cols')
- updated: float32 [2048, 2048], P('rows', 'cols')
Inputs may be any that keep to these rules, and one draw needn't show every extreme that they name: panel has full column rank and is well conditioned; rows and columns carry different scales.
All inputs are finite; a program needn't handle non-finite values.
Results may differ from a plain program's by a relative error of at most 0.0003.
Values sent between devices are 32-bit elements; how exact they have to be, the bound alone decides.
No kernel may reach another device: no remote copies, remote signals or barrier semaphores. Data moves between devices by JAX's collectives and lax.ppermute only.
A program may use at most 64 MiB of HBM per device.

v0:
```python
import jax
import jax.numpy as jnp
from jax import lax
from jax.sharding import PartitionSpec as P


def product(left, right):
    return jnp.dot(left, right, precision=lax.Precision.HIGHEST)


def lower_inverse_of(lower):
    identity = jnp.eye(lower.shape[0], dtype=lower.dtype)
    return jax.scipy.linalg.solve_triangular(lower, identity, lower=True)


def cholesky_pair(matrix):
    lower = jnp.linalg.cholesky(matrix)
    return (lower, lower_inverse_of(lower))


def gram_of(matrix):
    return lax.dot_general(
        matrix, matrix, (((0,), (0,)), ((), ())), precision=lax.Precision.HIGHEST
    )


def cross_of(panel_block, trailing):
    return lax.dot_general(
        panel_block, trailing, (((0,), (0,)), ((), ())), precision=lax.Precision.HIGHEST
    )


def finish_early(lower_inverse, cross_terms, panel_block, trailing):
    coefficients = product(lower_inverse, cross_terms)
    mixing = product(lower_inverse.T, coefficients)
    updated = trailing - product(panel_block, mixing)
    return (coefficients, updated)


def local(panel, trailing):
    panel_block = lax.all_gather(panel, "cols", axis=0, tiled=True)
    width = panel_block.shape[1]
    stacked = jnp.concatenate([gram_of(panel_block), cross_of(panel_block, trailing)], axis=1)
    summed = lax.psum(stacked, "rows")
    lower, lower_inverse = cholesky_pair(summed[:, :width])
    r_upper = lower.T
    cross_joint = summed[:, width:]
    coefficients, updated = finish_early(lower_inverse, cross_joint, panel_block, trailing)
    return (r_upper, coefficients, updated)


def solution(mesh):
    return jax.shard_map(
        local,
        mesh=mesh,
        in_specs=(P(("rows", "cols"), None), P("rows", "cols")),
        out_specs=(P(), P(None, "cols"), P("rows", "cols")),
        check_vma=False,
    )
```

profile of v0, /device:TPU:0, one launch (start us, length us, event | category | flops | bytes accessed | tf_op | source)
XLA Modules:
  0.0 156.2 jit_solution(14104111784305048921)
XLA Ops:
  7.2 16.0 %all_gather.3 = f32[256,256]{1,0:T(8,128)S(1)} all-gather(f32[64,256]{1,0:T(8,128)} %param.2), channel_id=1, replica_groups=mesh['rows'=8,'cols'=4] {'cols'}, dimensions={0}, use_global_device_ids=true | all-gather | bytes 327680 | tf_op jit(solution)/shard_map/all_gather | solution.py:41
  23.2 0.6 fusion.17
  23.8 1.0 fusion.18
  24.8 1.0 pad_maximum_fusion
  26.1 57.1 %all-reduce.3.cloned.1.call-done = f32[256,768]{0,1:T(8,128)} async-done(((f32[256,768]{0,1:T(8,128)}), f32[256,768]{0,1:T(8,128)}) %all-reduce.3.cloned.1.call-update) | async-done | bytes 786448 | tf_op jit(solution)/shard_map/psum | solution.py:44
  83.2 0.9 slice-done
  84.5 11.7 %cholesky.50 = f32[128,128]{1,0:T(8,128)S(1)} custom-call(f32[128,128]{1,0:T(8,128)S(1)} %cholesky.118), custom_call_target="Cholesky" | custom-call | tf_op jit(solution)/shard_map/jit(cholesky)/cholesky | solution.py:17
  96.2 9.8 %custom-call.15 = f32[1,128,128]{1,2,0:T(8,128)S(1)} custom-call(f32[1,128,128]{2,1,0:T(8,128)S(1)} %get-tuple-element.29), custom_call_target="InvertDiagBlocksLowerTriangular" | custom-call | tf_op jit(solution)/shard_map/jit(cholesky)/cholesky | solution.py:17
  106.3 0.3 convolution_subtract_fusion.1
  106.5 11.9 %cholesky.105 = f32[128,128]{1,0:T(8,128)S(1)} custom-call(f32[128,128]{1,0:T(8,128)S(1)} %convolution_subtract_fusion.1), custom_call_target="Cholesky" | custom-call | tf_op jit(solution)/shard_map/jit(cholesky)/cholesky | solution.py:17
  118.5 0.6 compare_reduce_fusion
  120.5 4.0 %while.1 = (s32[]{:T(128)}, f32[256,256]{1,0:T(8,128)S(1)}, s32[2,2]{1,0:T(2,128)S(1)}, f32[2,128,128]{2,1,0:T(8,128)S(1)}, s32[]{:T(128)}) while((s32[]{:T(128)}, f32[256,256]{1,0:T(8,128)S(1)}, s32[2,2]{1,0:T(2,128)S(1)}, f32[2,128,128]{2,1,0:T(8,128)S(1)}, s32[]{:T(128)}) %tuple.29), condition=%wide.while_cond, body=%wide.while_body.sunk | while | flops 2 | bytes 131181 | solution.py:13
  120.5 0.6 fusion.31
  121.1 1.4 bitcast_dynamic-update-slice_fusion.2
  122.5 0.6 fusion.31
  123.1 1.4 bitcast_dynamic-update-slice_fusion.2
  124.5 19.7 %custom-call.16 = f32[2,128,128]{1,2,0:T(8,128)S(1)} custom-call(f32[2,128,128]{2,1,0:T(8,128)S(1)} %get-tuple-element.10), custom_call_target="InvertDiagBlocksLowerTriangular" | custom-call | tf_op jit(solution)/shard_map/jit(_solve_triangular)/triangular_solve | solution.py:13
  144.2 0.3 fusion.7
  144.7 0.3 fusion.10
  145.0 0.6 fusion.1
  145.7 0.6 fusion.6
  146.5 1.0 fusion
  147.5 1.0 copy.9
  148.5 0.8 copy.8
  (25 shorter events, 1.4 us)
Async XLA Ops:
  7.2 16.7 %copy-start = (f32[256,512]{1,0:T(8,128)S(1)}, f32[256,512]{1,0:T(8,128)}, u32[]{:S(2)}) copy-start(f32[256,512]{1,0:T(8,128)} %param.3) | copy-start | bytes 1572868
  7.2 76.0 %all-reduce.3.cloned.1.call-start = ((), (), s32[]{:S(2)}) async-start(), calls=%async_computation | async-start | bytes 1572864 | tf_op jit(solution)/shard_map/psum | solution.py:44
  83.2 0.9 slice-start
  83.2 1.2 copy-start.2
  145.7 0.8 copy-start.1
Sparse Core Ops, SparseCore 0:
  25.9 57.1 all-reduce.2
where the time goes:
time: 156 us
  waiting for transfers between devices  57.1 us (37%)
  other arithmetic  54.9 us (35%)
  blocking collectives  16 us (10%)
  between operations  15.5 us (10%)
  local copies, waits for them, and re-layouts  7.43 us (5%)
  matrix products  5.19 us (3%)
    psum x1, waiting for transfers between devices, local(): summed = lax.psum(stacked, 'rows')  57.1 us
    another operation x6, other arithmetic, cholesky_pair(): lower = jnp.linalg.cholesky(matrix)  34.1 us
    another operation x3, other arithmetic, lower_inverse_of(): return jax.scipy.linalg.solve_triangular(lower, identity, lower=True)  19.7 us
    all_gather x1, blocking collectives, local(): panel_block = lax.all_gather(panel, 'cols', axis=0, tiled=True)  16 us
    another operation x6, local copies, waits for them, and re-layouts  3.95 us
  transfers between devices with their start and end apart: 1, of which 1 were waited for; matrix products, arithmetic and copies ran while one was open for 0% of the time, Pallas kernels for 0%

commit v1 on v0

--- a/solution.py
+++ b/solution.py
@@ -41,7 +41,8 @@
     panel_block = lax.all_gather(panel, "cols", axis=0, tiled=True)
     width = panel_block.shape[1]
     stacked = jnp.concatenate([gram_of(panel_block), cross_of(panel_block, trailing)], axis=1)
-    summed = lax.psum(stacked, "rows")
+    parts = lax.all_gather(stacked, "rows")
+    summed = jnp.sum(parts, axis=0)
     lower, lower_inverse = cholesky_pair(summed[:, :width])
     r_upper = lower.T
     cross_joint = summed[:, width:]

time: 156 us -> 149 us (0.955)
  waiting for transfers between devices: 57.1 us -> 45.8 us
  other arithmetic: 54.9 us -> 58 us
    psum x1 -> x0, waiting for transfers between devices: 57.1 us -> none  [local(): summed = lax.psum(stacked, 'rows')]
    all_gather x0 -> x1, waiting for transfers between devices: none -> 45.8 us  [local(): parts = lax.all_gather(stacked, 'rows')]
    reduce_sum x0 -> x1, other arithmetic: none -> 3.24 us  [local(): summed = jnp.sum(parts, axis=0)]
    unnamed x9 -> x6, local copies, waits for them, and re-layouts: 2.31 us -> 3.21 us
  transfers between devices with their start and end apart: 1 -> 1, of which waited for: 1 -> 1; matrix products, arithmetic and copies ran while one was open for 0% -> 1% of each run, Pallas kernels for 0% -> 0%
where the time goes in v1:
time: 149 us; the launch traced here: 148 us
  other arithmetic  58 us (39%)
  waiting for transfers between devices  45.8 us (31%)
  blocking collectives  15.9 us (11%)
  between operations  15.5 us (10%)
  local copies, waits for them, and re-layouts  7.27 us (5%)
  matrix products  5.87 us (4%)
    all_gather x1, waiting for transfers between devices, local(): parts = lax.all_gather(stacked, 'rows')  45.8 us
    another operation x6, other arithmetic, cholesky_pair(): lower = jnp.linalg.cholesky(matrix)  34.1 us
    another operation x3, other arithmetic, lower_inverse_of(): return jax.scipy.linalg.solve_triangular(lower, identity, lower=True)  19.7 us
    all_gather x1, blocking collectives, local(): panel_block = lax.all_gather(panel, 'cols', axis=0, tiled=True)  15.9 us
    another operation x6, local copies, waits for them, and re-layouts  3.95 us
    reduce_sum x1, other arithmetic, local(): summed = jnp.sum(parts, axis=0)  3.24 us
    unnamed x6, local copies, waits for them, and re-layouts  3.21 us
  transfers between devices with their start and end apart: 1, of which 1 were waited for; matrix products, arithmetic and copies ran while one was open for 1% of the time, Pallas kernels for 0%

profile of v1, /device:TPU:0, one launch (start us, length us, event | category | flops | bytes accessed | tf_op | source)
XLA Modules:
  0.0 148.4 jit_solution(990278376439506469)
XLA Ops:
  7.2 15.9 %all_gather.9 = f32[256,256]{1,0:T(8,128)S(1)} all-gather(f32[64,256]{1,0:T(8,128)} %param.2), channel_id=1, replica_groups=mesh['rows'=8,'cols'=4] {'cols'}, dimensions={0}, use_global_device_ids=true | all-gather | bytes 327680 | tf_op jit(solution)/shard_map/all_gather | solution.py:41
  23.1 0.6 fusion.17
  23.7 1.7 %fusion.18 = f32[256,512]{1,0:T(8,128)S(1)} fusion(f32[256,256]{1,0:T(8,128)S(1)} %all_gather.9, f32[256,512]{1,0:T(8,128)} %param.3), kind=kOutput, calls=%fused_computation.41 | convolution fusion | flops 402653184 | bytes 1310720 | tf_op jit(solution)/shard_map/dot_general | solution.py:28
  25.4 0.9 pad_maximum_fusion
  26.3 1.2 copy.13
  27.6 45.8 %all-gather.3.cloned.1.call-done = f32[2048,768]{1,0:T(8,128)} async-done(((f32[256,768]{1,0:T(8,128)}), f32[2048,768]{1,0:T(8,128)}) %all-gather.3.cloned.1.call-update) | async-done | bytes 6291472 | tf_op jit(solution)/shard_map/all_gather | solution.py:44
  73.4 3.2 %reduce_sum.9 = f32[256,768]{1,0:T(8,128)S(1)} reduce(f32[8,256,768]{2,1,0:T(8,128)} %bitcast.45, f32[]{:T(128)} %constant.75.clone.1), dimensions={0}, to_apply=%region_0.0 | reduce | flops 1376256 | bytes 7077892 | tf_op jit(solution)/shard_map/reduce_sum | solution.py:45
  76.9 11.7 %cholesky.50 = f32[128,128]{1,0:T(8,128)S(1)} custom-call(f32[128,128]{1,0:T(8,128)S(1)} %cholesky.118), custom_call_target="Cholesky" | custom-call | tf_op jit(solution)/shard_map/jit(cholesky)/cholesky | solution.py:17
  88.6 9.8 %custom-call.15 = f32[1,128,128]{1,2,0:T(8,128)S(1)} custom-call(f32[1,128,128]{2,1,0:T(8,128)S(1)} %get-tuple-element.32), custom_call_target="InvertDiagBlocksLowerTriangular" | custom-call | tf_op jit(solution)/shard_map/jit(cholesky)/cholesky | solution.py:17
  98.7 0.3 convolution_subtract_fusion.1
  98.9 11.8 %cholesky.105 = f32[128,128]{1,0:T(8,128)S(1)} custom-call(f32[128,128]{1,0:T(8,128)S(1)} %convolution_subtract_fusion.1), custom_call_target="Cholesky" | custom-call | tf_op jit(solution)/shard_map/jit(cholesky)/cholesky | solution.py:17
  110.8 0.6 compare_reduce_fusion
  112.9 4.0 %while.1 = (s32[]{:T(128)}, f32[256,256]{1,0:T(8,128)S(1)}, s32[2,2]{1,0:T(2,128)S(1)}, f32[2,128,128]{2,1,0:T(8,128)S(1)}, s32[]{:T(128)}) while((s32[]{:T(128)}, f32[256,256]{1,0:T(8,128)S(1)}, s32[2,2]{1,0:T(2,128)S(1)}, f32[2,128,128]{2,1,0:T(8,128)S(1)}, s32[]{:T(128)}) %tuple.30), condition=%wide.while_cond, body=%wide.while_body.sunk | while | flops 2 | bytes 131181 | solution.py:13
  112.9 0.6 fusion.31
  113.5 1.4 bitcast_dynamic-update-slice_fusion.2
  114.9 0.6 fusion.31
  115.5 1.4 bitcast_dynamic-update-slice_fusion.2
  116.9 19.7 %custom-call.16 = f32[2,128,128]{1,2,0:T(8,128)S(1)} custom-call(f32[2,128,128]{2,1,0:T(8,128)S(1)} %get-tuple-element.10), custom_call_target="InvertDiagBlocksLowerTriangular" | custom-call | tf_op jit(solution)/shard_map/jit(_solve_triangular)/triangular_solve | solution.py:13
  137.1 0.3 fusion.10
  137.4 0.6 fusion.1
  138.1 0.6 fusion.6
  138.7 1.0 fusion
  139.8 1.0 copy.15
  140.8 0.8 copy.14
  (21 shorter events, 1.2 us)
Async XLA Ops:
  7.2 66.2 %all-gather.3.cloned.1.call-start = ((), (), s32[]{:S(2)}) async-start(), calls=%async_computation | async-start | bytes 7077888 | tf_op jit(solution)/shard_map/all_gather | solution.py:44
  138.1 3.5 %copy-start = (f32[256,512]{1,0:T(8,128)}, f32[256,512]{1,0:T(8,128)S(1)}, u32[]{:S(2)}) copy-start(f32[256,512]{1,0:T(8,128)S(1)} %fusion.1) | copy-start | bytes 1572868
Sparse Core Ops, SparseCore 0:
  26.4 46.9 all-gather.2
